TPU v7x, 32 devices: a whole 2x2x4 slice. The times are simulated.
32 devices in a mesh: grp: 2 (over y), seq: 4 (over z), head: 2 (over x), sub: 2 (over core).
Axes of the slice: x: 2, y: 2, z: 4, core: 2. Of those that a mesh axis runs over, the one named last changes fastest.
Arguments:
- queries: float32 [1536, 2048], P(('grp', 'seq'), ('head', 'sub')), parts along dimension 0, may hold values from -6 to 6
- keys: float32 [1536, 2048], P(('grp', 'seq'), ('head', 'sub')), parts along dimension 0, may hold values from -6 to 6
- values: float32 [1536, 2048], P(('grp', 'seq'), ('head', 'sub')), parts along dimension 0, may hold values from -40 to 40
- opt_queries: float32 [16, 64, 2048], P(('grp', 'seq'), None, ('head', 'sub')), parts along dimension 0, may hold values from -6 to 6
- opt_keys: float32 [16, 64, 2048], P(('grp', 'seq'), None, ('head', 'sub')), parts along dimension 0, may hold values from -6 to 6
- opt_values: float32 [16, 64, 2048], P(('grp', 'seq'), None, ('head', 'sub')), parts along dimension 0, may hold values from -40 to 40
- opt_offsets: int32 [16], P(('grp', 'seq')), parts along dimension 0, may hold values from 0 to 192
- opt_lengths: int32 [16], P(('grp', 'seq')), parts along dimension 0, may hold values from 1 to 64, 320 in all
- norm_gain: float32 [2048], P(('head', 'sub')), may hold values from 0.5 to 2
- out_weight: bfloat16 [2048, 4096], P(('head', 'sub')), may hold values from -0.125 to 0.125
Outputs:
- ctx_out: bfloat16 [1536, 4096], P(('grp', 'seq'), ('head', 'sub')), parts along dimension 0
- opt_out: bfloat16 [16, 64, 4096], P(('grp', 'seq'), None, ('head', 'sub')), parts along dimension 0
There are 2 independent parts, one for each index of `grp`. A program takes and returns all parts, laid end to end along the dimension named above; an argument that names none is the same for every part. Nothing has to cross between parts.
Inputs may be any that keep to these rules, and one draw needn't show every extreme that they name: `opt_lengths`: within each scoring group the 8 lengths sum to 320, and the longest option of each group has exactly 64 tokens in every draw.
All inputs are finite; a program needn't handle non-finite values.
Results may differ from a plain program's by a relative error of at most 0.017.
Values may be sent and summed in bfloat16 or wider, within the bound.
A program may use at most 64 MiB of HBM per device.

v0:
```python
import jax
import jax.numpy as jnp
from jax import lax
from jax.sharding import PartitionSpec as P

DH = 128
norm_epsilon = 1e-05


def entering(value, axis, join, neutral):
    place = lax.axis_index(axis)
    gathered = lax.all_gather(value.astype(jnp.bfloat16), axis)
    state = jnp.zeros_like(value) + jnp.asarray(neutral, value.dtype)

    def one(hop, state):
        return join(state, lax.dynamic_index_in_dim(gathered, hop, 0, False).astype(value.dtype))

    return lax.fori_loop(0, place, one, state)


def head_norm(attended, gain, mask):
    mean_square = jnp.mean(attended * attended, axis=-1, keepdims=True)
    return (attended * lax.rsqrt(mean_square + norm_epsilon) * gain * mask).astype(jnp.bfloat16)


def combine_sum(earlier, later):
    return earlier + later


def grouped_project(rows, weight_columns, groups):
    count = rows.shape[0]
    flat = rows.reshape(count, groups, rows.shape[1] // groups)
    weight_groups = weight_columns.reshape(
        groups, weight_columns.shape[0] // groups, weight_columns.shape[1]
    )
    partial_value = jnp.einsum(
        "rgk,gkd->grd", flat, weight_groups, preferred_element_type=jnp.float32
    )
    partial_value = lax.optimization_barrier(partial_value.astype(jnp.bfloat16)).astype(jnp.float32)
    return jnp.sum(partial_value, axis=0).astype(jnp.bfloat16)


def on_device(
    queries,
    keys,
    values,
    opt_queries,
    opt_keys,
    opt_values,
    opt_offsets,
    opt_lengths,
    norm_gain,
    out_weight,
):
    highest = lax.Precision.HIGHEST
    tok_rows = queries.shape[0]
    heads = queries.shape[1] // DH
    opt_count = opt_queries.shape[0]
    slot_count = opt_queries.shape[1]
    group_count = lax.axis_size(("head", "sub"))
    weight_columns = lax.all_to_all(
        out_weight, ("head", "sub"), split_axis=1, concat_axis=0, tiled=True
    )
    block_q = queries.reshape(tok_rows, heads, DH)
    block_k = keys.reshape(tok_rows, heads, DH)
    block_v = values.reshape(tok_rows, heads, DH)
    gain = norm_gain.reshape(heads, DH)
    states = jnp.einsum("thd,the->hde", block_k, block_v, precision=highest)
    positions = jnp.arange(tok_rows, dtype=jnp.int32)
    causal = (positions[:, None] >= positions[None, :]).astype(jnp.float32)
    scores = jnp.einsum("thd,shd->hts", block_q, block_k, precision=highest) * causal[None]
    intra = jnp.einsum("hts,she->the", scores, block_v, precision=highest)
    opt_q = opt_queries.reshape(opt_count, slot_count, heads, DH)
    opt_k = opt_keys.reshape(opt_count, slot_count, heads, DH)
    opt_v = opt_values.reshape(opt_count, slot_count, heads, DH)
    before = (positions[None, :] < opt_offsets[:, None]).astype(jnp.float32)
    local = jnp.einsum("ot,thd,the->ohde", before, block_k, block_v, precision=highest)
    slots = jnp.arange(slot_count, dtype=jnp.int32)
    slot_causal = (slots[:, None] >= slots[None, :]).astype(jnp.float32)
    opt_scores = (
        jnp.einsum("oihd,ojhd->ohij", opt_q, opt_k, precision=highest) * slot_causal[None, None]
    )
    opt_intra = jnp.einsum("ohij,ojhe->oihe", opt_scores, opt_v, precision=highest)
    prefix = entering(states, "seq", combine_sum, jnp.zeros_like(states))
    inter = jnp.einsum("thd,hde->the", block_q, prefix, precision=highest)
    context_normed = head_norm(inter + intra, gain, 1.0).reshape(tok_rows, heads * DH)
    opt_state = prefix[None] + local
    opt_inter = jnp.einsum("oihd,ohde->oihe", opt_q, opt_state, precision=highest)
    valid = (slots[None, :] < opt_lengths[:, None]).astype(jnp.float32)
    opt_normed = head_norm(opt_inter + opt_intra, gain, valid[:, :, None, None]).reshape(
        opt_count * slot_count, heads * DH
    )
    gathered_ctx, gathered_opt = (
        lax.all_gather(context_normed, ("head", "sub"), axis=1, tiled=True),
        lax.all_gather(opt_normed, ("head", "sub"), axis=1, tiled=True),
    )
    context_out = grouped_project(gathered_ctx, weight_columns, group_count)
    opt_rows = grouped_project(gathered_opt, weight_columns, group_count)
    option_out = opt_rows.reshape(opt_count, slot_count, opt_rows.shape[1])
    return (context_out, option_out)


def solution(mesh):
    placed = (
        P(("grp", "seq"), ("head", "sub")),
        P(("grp", "seq"), ("head", "sub")),
        P(("grp", "seq"), ("head", "sub")),
        P(("grp", "seq"), None, ("head", "sub")),
        P(("grp", "seq"), None, ("head", "sub")),
        P(("grp", "seq"), None, ("head", "sub")),
        P(("grp", "seq")),
        P(("grp", "seq")),
        P(("head", "sub")),
        P(("head", "sub"), None),
    )
    return jax.shard_map(
        on_device,
        mesh=mesh,
        in_specs=placed,
        out_specs=(P(("grp", "seq"), ("head", "sub")), P(("grp", "seq"), None, ("head", "sub"))),
        check_vma=False,
    )
```

profile of v0, /device:TPU:0, one launch (start us, length us, event | category | flops | bytes accessed | tf_op | source)
XLA Modules:
  0.0 91.5 jit_solution(10964770409362976219)
XLA Ops:
  0.6 0.0 copy-start
  0.6 6.5 %copy.40 = bf16[512,4096]{0,1:T(8,128)(2,1)} copy(bf16[512,4096]{1,0:T(8,128)(2,1)} %param.21) | data formatting | bytes 8388608 | tf_op args[9]
  7.2 6.3 %copy.41 = bf16[512,4,1024]{2,0,1:T(8,128)(2,1)} copy(bf16[512,4,1024]{0,2,1:T(8,128)(2,1)} %bitcast.132) | data formatting | bytes 8388608 | tf_op jit(solution)/shard_map/all_to_all | solution.py:61
  13.5 5.0 %all-to-all-start = ((bf16[512,4,1024]{2,0,1:T(8,128)(2,1)}), bf16[512,4,1024]{2,0,1:T(8,128)(2,1)}, u32[]{:S(2)}, u32[]{:S(2)}) async-start(bf16[512,4,1024]{2,0,1:T(8,128)(2,1)} %copy.41), calls=%async_computation | async-start | bytes 8388608 | tf_op jit(solution)/shard_map/all_to_all | solution.py:61
  18.5 0.0 copy-start.8
  18.5 0.0 copy-start.4
  18.5 0.0 copy-start.5
  18.5 0.0 copy-start.9
  18.6 0.0 copy-start.6
  18.6 1.1 %convolution_convert_fusion = bf16[4,128,128]{2,1,0:T(8,128)(2,1)S(1)} fusion(f32[192,512]{1,0:T(8,128)S(1)} %copy-done.1, f32[192,512]{1,0:T(8,128)S(1)} %copy-done), kind=kOutput, calls=%fused_computation.17 | convolution fusion | flops 151060480 | bytes 917504 | tf_op jit(solution)/shard_map/thd,the->hde/dot_general | solution.py:68
  19.7 17.9 %all-gather = bf16[16,128,128]{2,1,0:T(8,128)(2,1)S(1)} all-gather(bf16[4,128,128]{2,1,0:T(8,128)(2,1)S(1)} %convolution_convert_fusion), channel_id=2, replica_groups=mesh['grp'=2,'seq'=4,'head'=2,'sub'=2] {'seq'}, dimensions={0}, use_global_device_ids=true | all-gather | bytes 655360 | tf_op jit(solution)/shard_map/all_gather | solution.py:12
  37.6 0.0 copy-start.3
  37.6 0.1 fusion.39
  37.7 0.5 convolution_multiply_fusion.1
  38.3 0.1 compare_convert_fusion.1
  38.4 1.9 %fusion.10 = f32[2,4,128,128]{3,2,1,0:T(8,128)S(1)} fusion(f32[192,4,128]{2,0,1:T(8,128)S(1)} %copy_bitcast_fusion, f32[192,2]{0,1:T(2,128)S(1)} %fusion.39, f32[4,128,128]{2,1,0:T(8,128)S(1)} %get-tuple-element.25, f32[192,512]{1,0:T(8,128)S(1)} %copy-done.1), kind=kOutput, calls=%fused_computation.9 | convolution fusion | flops 302317568 | bytes 1574400 | tf_op jit(solution)/shard_map/ot,thd,the->ohde/dot_general | solution.py:77
  40.3 0.6 convolution_bitcast_fusion.3
  40.9 0.5 multiply_reduce_fusion.1
  41.4 0.2 multiply_convert_fusion.1
  41.6 0.1 copy.49
  41.7 29.2 %all_gather.15 = bf16[128,2048]{1,0:T(8,128)(2,1)S(1)} all-gather(bf16[128,512]{1,0:T(8,128)(2,1)S(1)} %bitcast.136), channel_id=1, replica_groups=mesh['grp'=2,'seq'=4,'head'=2,'sub'=2] {'head','sub'}, dimensions={1}, use_global_device_ids=true | all-gather | bytes 655360 | tf_op jit(solution)/shard_map/all_gather | solution.py:95
  70.9 1.0 %copy.50 = bf16[128,2048]{0,1:T(8,128)(2,1)} copy(bf16[128,2048]{1,0:T(8,128)(2,1)S(1)} %all_gather.15) | data formatting | bytes 1048576 | tf_op jit(solution)/shard_map/all_gather | solution.py:95
  72.0 0.5 convolution_bitcast_fusion.1
  72.5 0.8 convolution_multiply_fusion
  73.3 1.0 %multiply_reduce_fusion = (f32[192,4]{0,1:T(4,128)S(1)}, f32[192,4,128]{2,0,1:T(8,128)S(1)}) fusion(f32[192,4,128]{2,0,1:T(8,128)S(1)} %convolution_bitcast_fusion.1, f32[4,192,192]{2,1,0:T(8,128)S(1)} %convolution_multiply_fusion, f32[192,512]{1,0:T(8,128)S(1)} %copy-done.1), kind=kOutput, calls=%fused_computation.31 | convolution fusion | flops 226786560 | bytes 1772544 | tf_op jit(solution)/shard_map/hts,she->the/dot_general | solution.py:72
  74.3 0.2 copy_bitcast_fusion.1
  74.5 8.7 %all_gather.14 = bf16[192,2048]{1,0:T(8,128)(2,1)S(1)} all-gather(bf16[192,512]{1,0:T(8,128)(2,1)S(1)} %copy_bitcast_fusion.1), channel_id=1, replica_groups=mesh['grp'=2,'seq'=4,'head'=2,'sub'=2] {'head','sub'}, dimensions={1}, use_global_device_ids=true | all-gather | bytes 983040 | tf_op jit(solution)/shard_map/all_gather | solution.py:94
  83.2 0.0 all-to-all-done
  83.2 3.2 %fusion.4 = bf16[4,192,1024]{2,1,0:T(8,128)(2,1)S(1)} fusion(bf16[512,4,1024]{2,0,1:T(8,128)(2,1)} %all-to-all-done, bf16[24,4,8,512]{3,2,1,0:T(8,128)(2,1)S(1)} %bitcast.133), kind=kOutput, calls=%fused_computation.5 | convolution fusion | flops 806092800 | bytes 6553600 | tf_op jit(solution)/shard_map/rgk,gkd->grd/dot_general | solution.py:36
  86.4 3.0 %fusion.7 = bf16[4,128,1024]{2,1,0:T(8,128)(2,1)S(1)} fusion(bf16[128,4,512]{0,2,1:T(8,128)(2,1)S(1)} %bitcast.134, bf16[512,4,1024]{2,0,1:T(8,128)(2,1)} %all-to-all-done), kind=kOutput, calls=%fused_computation.6 | convolution fusion | flops 537395200 | bytes 5767168 | tf_op jit(solution)/shard_map/rgk,gkd->grd/dot_general | solution.py:36
  89.4 1.1 %reduce_sum.43 = bf16[192,1024]{1,0:T(8,128)(2,1)} reduce(bf16[4,192,1024]{2,1,0:T(8,128)(2,1)S(1)} %fusion.4, bf16[]{:T(256)} %constant.28.clone.1), dimensions={0}, to_apply=%region_3.4 | reduce | flops 589824 | bytes 1966082 | tf_op jit(solution)/shard_map/reduce_sum | solution.py:40
  90.6 0.9 %reduce_sum.45 = bf16[128,1024]{1,0:T(8,128)(2,1)} reduce(bf16[4,128,1024]{2,1,0:T(8,128)(2,1)S(1)} %fusion.7, bf16[]{:T(256)} %constant.28.clone.1), dimensions={0}, to_apply=%region_5.6 | reduce | flops 393216 | bytes 1310722 | tf_op jit(solution)/shard_map/reduce_sum | solution.py:40
  (21 shorter events, 0.1 us)
Async XLA Ops:
  0.6 17.9 %copy-start = (f32[192,512]{1,0:T(8,128)S(1)}, f32[192,512]{1,0:T(8,128)}, u32[]{:S(2)}) copy-start(f32[192,512]{1,0:T(8,128)} %param.13) | copy-start | bytes 1179652
  13.5 5.1 %copy-start.1 = (f32[192,512]{1,0:T(8,128)S(1)}, f32[192,512]{1,0:T(8,128)}, u32[]{:S(2)}) copy-start(f32[192,512]{1,0:T(8,128)} %param.14) | copy-start | bytes 1179652
  13.5 69.7 %all-to-all-start = ((bf16[512,4,1024]{2,0,1:T(8,128)(2,1)}), bf16[512,4,1024]{2,0,1:T(8,128)(2,1)}, u32[]{:S(2)}, u32[]{:S(2)}) async-start(bf16[512,4,1024]{2,0,1:T(8,128)(2,1)} %copy.41), calls=%async_computation | async-start | bytes 8388608 | tf_op jit(solution)/shard_map/all_to_all | solution.py:61
  18.5 19.1 %copy-start.8 = (s32[2]{0:T(128)S(1)}, s32[2]{0:T(128)}, u32[]{:S(2)}) copy-start(s32[2]{0:T(128)} %param.18) | copy-start | bytes 28
  18.5 19.2 %copy-start.4 = (f32[2,64,512]{2,1,0:T(8,128)S(1)}, f32[2,64,512]{2,1,0:T(8,128)}, u32[]{:S(2)}) copy-start(f32[2,64,512]{2,1,0:T(8,128)} %param.15) | copy-start | bytes 786436
  18.5 19.2 %copy-start.5 = (f32[2,64,512]{2,1,0:T(8,128)S(1)}, f32[2,64,512]{2,1,0:T(8,128)}, u32[]{:S(2)}) copy-start(f32[2,64,512]{2,1,0:T(8,128)} %param.16) | copy-start | bytes 786436
  18.5 19.8 %copy-start.9 = (s32[2]{0:T(128)S(1)}, s32[2]{0:T(128)}, u32[]{:S(2)}) copy-start(s32[2]{0:T(128)} %param.19) | copy-start | bytes 28
  18.6 22.2 %copy-start.6 = (f32[2,64,512]{2,1,0:T(8,128)S(1)}, f32[2,64,512]{2,1,0:T(8,128)}, u32[]{:S(2)}) copy-start(f32[2,64,512]{2,1,0:T(8,128)} %param.17) | copy-start | bytes 786436
  37.6 3.8 %copy-start.7 = (f32[512]{0:T(512)S(1)}, f32[512]{0:T(512)}, u32[]{:S(2)}) copy-start(f32[512]{0:T(512)} %param.20) | copy-start | bytes 6148
  37.6 34.4 %copy-start.3 = (f32[192,512]{1,0:T(8,128)S(1)}, f32[192,512]{1,0:T(8,128)}, u32[]{:S(2)}) copy-start(f32[192,512]{1,0:T(8,128)} %param.12) | copy-start | bytes 1179652
  83.2 3.2 %copy-start.2 = (bf16[128,2048]{0,1:T(8,128)(2,1)S(1)}, bf16[128,2048]{0,1:T(8,128)(2,1)}, u32[]{:S(2)}) copy-start(bf16[128,2048]{0,1:T(8,128)(2,1)} %copy.50) | copy-start | bytes 1572868
where the time goes:
time: 92 us; the launch traced here: 91.5 us
  blocking collectives  55.8 us (61%)
  local copies, waits for them, and re-layouts  14.1 us (15%)
  matrix products  13.1 us (14%)
  starting transfers between devices  4.97 us (5%)
  other arithmetic  2.58 us (3%)
    all_gather x1, blocking collectives, on_device(): lax.all_gather(opt_normed, ('head', 'sub'), axis=1, tiled=True)  29.2 us
    all_gather x1, blocking collectives, entering(): gathered = lax.all_gather(value.astype(jnp.bfloat16), axis)  17.9 us
    all_gather x1, blocking collectives, on_device(): lax.all_gather(context_normed, ('head', 'sub'), axis=1, tiled=True)  8.71 us
    unnamed x22, local copies, waits for them, and re-layouts  6.62 us
    all_to_all x1, local copies, waits for them, and re-layouts, on_device(): lax.all_to_all(out_weight, ('head', 'sub'), split_axis=1, concat_axis=0,...  6.33 us
    dot_general x2, matrix products, grouped_project(): jnp.einsum('rgk,gkd->grd', flat, weight_groups, preferred_element_type=jn...  6.22 us
    all_to_all x1, starting transfers between devices, on_device(): lax.all_to_all(out_weight, ('head', 'sub'), split_axis=1, concat_axis=0,...  4.97 us
    reduce_sum x2, other arithmetic, grouped_project(): return jnp.sum(partial_value, axis=0).astype(jnp.bfloat16)  2.06 us
  transfers between devices with their start and end apart: 1, of which 0 were waited for; matrix products, arithmetic and copies ran while one was open for 9% of the time, Pallas kernels for 0%

commit v1 on v0

--- a/solution.py
+++ b/solution.py
@@ -91,7 +91,7 @@
         opt_count * slot_count, heads * DH
     )
     gathered_ctx, gathered_opt = (
-        lax.all_gather(context_normed, ("head", "sub"), axis=1, tiled=True),
+        jnp.concatenate(jax.lax.all_gather(context_normed, ("head", "sub")), axis=1),
         lax.all_gather(opt_normed, ("head", "sub"), axis=1, tiled=True),
     )
     context_out = grouped_project(gathered_ctx, weight_columns, group_count)

time: 92 us -> 88.7 us (0.964)
  blocking collectives: 55.8 us -> 53.1 us
    all_gather x1, blocking collectives: 29.2 us -> 26.5 us  [on_device(): lax.all_gather(opt_normed, ('head', 'sub'), axis=1, tiled=True)]
    unnamed x22 -> x20, local copies, waits for them, and re-layouts: 6.62 us -> 6.66 us
where the time goes in v1:
time: 88.7 us; the launch traced here: 88.1 us
  blocking collectives  53.1 us (60%)
  local copies, waits for them, and re-layouts  13.6 us (15%)
  matrix products  13 us (15%)
  starting transfers between devices  4.98 us (6%)
  other arithmetic  2.57 us (3%)
  between operations  0.93 us (1%)
    all_gather x1, blocking collectives, on_device(): lax.all_gather(opt_normed, ('head', 'sub'), axis=1, tiled=True)  26.5 us
    all_gather x1, blocking collectives, entering(): gathered = lax.all_gather(value.astype(jnp.bfloat16), axis)  17.9 us
    all_gather x1, blocking collectives, on_device(): jax.lax.all_gather(context_normed, ('head', 'sub'))  8.71 us
    unnamed x20, local copies, waits for them, and re-layouts  6.66 us
    all_to_all x1, local copies, waits for them, and re-layouts, on_device(): lax.all_to_all(out_weight, ('head', 'sub'), split_axis=1, concat_axis=0,...  6.29 us
    dot_general x2, matrix products, grouped_project(): jnp.einsum('rgk,gkd->grd', flat, weight_groups, preferred_element_type=jn...  6.14 us
    all_to_all x1, starting transfers between devices, on_device(): lax.all_to_all(out_weight, ('head', 'sub'), split_axis=1, concat_axis=0,...  4.98 us
    reduce_sum x2, other arithmetic, grouped_project(): return jnp.sum(partial_value, axis=0).astype(jnp.bfloat16)  2.06 us
  transfers between devices with their start and end apart: 1, of which 0 were waited for; matrix products, arithmetic and copies ran while one was open for 9% of the time, Pallas kernels for 0%

profile of v1, /device:TPU:0, one launch (start us, length us, event | category | flops | bytes accessed | tf_op | source)
XLA Modules:
  0.0 88.1 jit_solution(190686780942967769)
XLA Ops:
  0.6 0.0 copy-start
  0.6 6.6 %copy.39 = bf16[512,4096]{0,1:T(8,128)(2,1)} copy(bf16[512,4096]{1,0:T(8,128)(2,1)} %param.21) | data formatting | bytes 8388608 | tf_op args[9]
  7.2 6.3 %copy.40 = bf16[512,4,1024]{2,0,1:T(8,128)(2,1)} copy(bf16[512,4,1024]{0,2,1:T(8,128)(2,1)} %bitcast.126) | data formatting | bytes 8388608 | tf_op jit(solution)/shard_map/all_to_all | solution.py:61
  13.5 5.0 %all-to-all-start = ((bf16[512,4,1024]{2,0,1:T(8,128)(2,1)}), bf16[512,4,1024]{2,0,1:T(8,128)(2,1)}, u32[]{:S(2)}, u32[]{:S(2)}) async-start(bf16[512,4,1024]{2,0,1:T(8,128)(2,1)} %copy.40), calls=%async_computation | async-start | bytes 8388608 | tf_op jit(solution)/shard_map/all_to_all | solution.py:61
  18.6 1.1 %convolution_convert_fusion = bf16[4,128,128]{2,1,0:T(8,128)(2,1)S(1)} fusion(f32[192,512]{1,0:T(8,128)S(1)} %copy-done.1, f32[192,512]{1,0:T(8,128)S(1)} %copy-done), kind=kOutput, calls=%fused_computation.17 | convolution fusion | flops 151060480 | bytes 917504 | tf_op jit(solution)/shard_map/thd,the->hde/dot_general | solution.py:68
  19.6 17.9 %all-gather = bf16[16,128,128]{2,1,0:T(8,128)(2,1)S(1)} all-gather(bf16[4,128,128]{2,1,0:T(8,128)(2,1)S(1)} %convolution_convert_fusion), channel_id=2, replica_groups=mesh['grp'=2,'seq'=4,'head'=2,'sub'=2] {'seq'}, dimensions={0}, use_global_device_ids=true | all-gather | bytes 655360 | tf_op jit(solution)/shard_map/all_gather | solution.py:12
  37.6 0.0 copy-start.6
  37.6 0.0 copy-start.8
  37.6 0.0 copy-start.3
  37.6 0.0 copy-start.4
  37.6 0.5 convolution_bitcast_fusion.1
  38.1 0.8 convolution_multiply_fusion
  38.9 0.0 copy-start.5
  38.9 1.0 %multiply_reduce_fusion = (f32[192,4]{0,1:T(4,128)S(1)}, f32[192,4,128]{2,0,1:T(8,128)S(1)}) fusion(f32[192,4,128]{2,0,1:T(8,128)S(1)} %convolution_bitcast_fusion.1, f32[4,192,192]{2,1,0:T(8,128)S(1)} %convolution_multiply_fusion, f32[192,512]{1,0:T(8,128)S(1)} %copy-done.1), kind=kOutput, calls=%fused_computation.30 | convolution fusion | flops 226786560 | bytes 1772544 | tf_op jit(solution)/shard_map/hts,she->the/dot_general | solution.py:72
  39.9 0.2 multiply_convert_fusion
  40.1 0.2 copy.38
  40.3 0.1 all_gather_reshape.3
  40.4 0.1 compare_convert_fusion.1
  40.5 0.1 fusion.37
  40.6 0.5 convolution_multiply_fusion.1
  41.1 1.9 %fusion.10 = f32[2,4,128,128]{3,2,1,0:T(8,128)S(1)} fusion(f32[192,4,128]{2,0,1:T(8,128)S(1)} %copy_bitcast_fusion, f32[192,2]{0,1:T(2,128)S(1)} %fusion.37, f32[4,128,128]{2,1,0:T(8,128)S(1)} %get-tuple-element.25, f32[192,512]{1,0:T(8,128)S(1)} %copy-done.1), kind=kOutput, calls=%fused_computation.9 | convolution fusion | flops 302317568 | bytes 1574400 | tf_op jit(solution)/shard_map/ot,thd,the->ohde/dot_general | solution.py:77
  43.1 0.6 convolution_bitcast_fusion.3
  43.7 0.5 multiply_reduce_fusion.1
  44.2 0.2 multiply_convert_fusion.1
  44.3 0.1 copy.47
  44.5 26.5 %all_gather.15 = bf16[128,2048]{1,0:T(8,128)(2,1)S(1)} all-gather(bf16[128,512]{1,0:T(8,128)(2,1)S(1)} %bitcast.129), channel_id=1, replica_groups=mesh['grp'=2,'seq'=4,'head'=2,'sub'=2] {'head','sub'}, dimensions={1}, use_global_device_ids=true | all-gather | bytes 655360 | tf_op jit(solution)/shard_map/all_gather | solution.py:95
  70.9 0.3 copy.48
  71.2 8.7 %all_gather.14 = bf16[4,192,512]{2,1,0:T(8,128)(2,1)S(1)} all-gather(bf16[1,192,512]{2,1,0:T(8,128)(2,1)S(1)} %all_gather_reshape.3), channel_id=1, replica_groups=mesh['grp'=2,'seq'=4,'head'=2,'sub'=2] {'head','sub'}, dimensions={0}, use_global_device_ids=true | all-gather | bytes 983040 | tf_op jit(solution)/shard_map/all_gather | solution.py:94
  79.9 3.2 %fusion.4 = bf16[4,192,1024]{2,1,0:T(8,128)(2,1)S(1)} fusion(bf16[512,4,1024]{2,0,1:T(8,128)(2,1)} %all-to-all-done, bf16[4,192,512]{2,1,0:T(8,128)(2,1)S(1)} %all_gather.14), kind=kOutput, calls=%fused_computation.5 | convolution fusion | flops 806092800 | bytes 6553600 | tf_op jit(solution)/shard_map/rgk,gkd->grd/dot_general | solution.py:36
  83.1 3.0 %fusion.7 = bf16[4,128,1024]{2,1,0:T(8,128)(2,1)S(1)} fusion(bf16[128,4,512]{0,2,1:T(8,128)(2,1)S(1)} %bitcast.127, bf16[512,4,1024]{2,0,1:T(8,128)(2,1)} %all-to-all-done), kind=kOutput, calls=%fused_computation.6 | convolution fusion | flops 537395200 | bytes 5767168 | tf_op jit(solution)/shard_map/rgk,gkd->grd/dot_general | solution.py:36
  86.1 1.1 %reduce_sum.43 = bf16[192,1024]{1,0:T(8,128)(2,1)} reduce(bf16[4,192,1024]{2,1,0:T(8,128)(2,1)S(1)} %fusion.4, bf16[]{:T(256)} %constant.28.clone.1), dimensions={0}, to_apply=%region_3.4 | reduce | flops 589824 | bytes 1966082 | tf_op jit(solution)/shard_map/reduce_sum | solution.py:40
  87.2 0.9 %reduce_sum.45 = bf16[128,1024]{1,0:T(8,128)(2,1)} reduce(bf16[4,128,1024]{2,1,0:T(8,128)(2,1)S(1)} %fusion.7, bf16[]{:T(256)} %constant.28.clone.1), dimensions={0}, to_apply=%region_5.6 | reduce | flops 393216 | bytes 1310722 | tf_op jit(solution)/shard_map/reduce_sum | solution.py:40
  (21 shorter events, 0.1 us)
Async XLA Ops:
  0.6 17.9 %copy-start = (f32[192,512]{1,0:T(8,128)S(1)}, f32[192,512]{1,0:T(8,128)}, u32[]{:S(2)}) copy-start(f32[192,512]{1,0:T(8,128)} %param.13) | copy-start | bytes 1179652
  13.5 5.0 %copy-start.1 = (f32[192,512]{1,0:T(8,128)S(1)}, f32[192,512]{1,0:T(8,128)}, u32[]{:S(2)}) copy-start(f32[192,512]{1,0:T(8,128)} %param.14) | copy-start | bytes 1179652
  13.5 66.4 %all-to-all-start = ((bf16[512,4,1024]{2,0,1:T(8,128)(2,1)}), bf16[512,4,1024]{2,0,1:T(8,128)(2,1)}, u32[]{:S(2)}, u32[]{:S(2)}) async-start(bf16[512,4,1024]{2,0,1:T(8,128)(2,1)} %copy.40), calls=%async_computation | async-start | bytes 8388608 | tf_op jit(solution)/shard_map/all_to_all | solution.py:61
  18.5 19.1 %copy-start.2 = (f32[192,512]{1,0:T(8,128)S(1)}, f32[192,512]{1,0:T(8,128)}, u32[]{:S(2)}) copy-start(f32[192,512]{1,0:T(8,128)} %param.12) | copy-start | bytes 1179652
  37.6 2.4 %copy-start.6 = (f32[512]{0:T(512)S(1)}, f32[512]{0:T(512)}, u32[]{:S(2)}) copy-start(f32[512]{0:T(512)} %param.20) | copy-start | bytes 6148
  37.6 2.8 %copy-start.8 = (s32[2]{0:T(128)S(1)}, s32[2]{0:T(128)}, u32[]{:S(2)}) copy-start(s32[2]{0:T(128)} %param.19) | copy-start | bytes 28
  37.6 2.9 %copy-start.7 = (s32[2]{0:T(128)S(1)}, s32[2]{0:T(128)}, u32[]{:S(2)}) copy-start(s32[2]{0:T(128)} %param.18) | copy-start | bytes 28
  37.6 3.0 %copy-start.3 = (f32[2,64,512]{2,1,0:T(8,128)S(1)}, f32[2,64,512]{2,1,0:T(8,128)}, u32[]{:S(2)}) copy-start(f32[2,64,512]{2,1,0:T(8,128)} %param.15) | copy-start | bytes 786436
  37.6 3.0 %copy-start.4 = (f32[2,64,512]{2,1,0:T(8,128)S(1)}, f32[2,64,512]{2,1,0:T(8,128)}, u32[]{:S(2)}) copy-start(f32[2,64,512]{2,1,0:T(8,128)} %param.16) | copy-start | bytes 786436
  38.9 4.7 %copy-start.5 = (f32[2,64,512]{2,1,0:T(8,128)S(1)}, f32[2,64,512]{2,1,0:T(8,128)}, u32[]{:S(2)}) copy-start(f32[2,64,512]{2,1,0:T(8,128)} %param.17) | copy-start | bytes 786436
